TPU v7x, 32 devices: a whole 2x2x4 slice. The times are simulated.
32 devices in a mesh: frames: 4 (over y, core), bricks: 8 (over z, x).
Axes of the slice: x: 2, y: 2, z: 4, core: 2. Of those that a mesh axis runs over, the one named last changes fastest.
Arguments:
- positions: float32 [3, 8, 16384], P(None, 'frames', 'bricks'), may hold values from 0 to 1
- counts: int32 [8, 8], P('frames'), may hold values from 1 to 2048, as said below
- kvec_x: int32 [128], replicated, may hold values from 1 to 64
- kvec_y: int32 [128], replicated, may hold values from 1 to 64
- kvec_z: int32 [8], replicated, may hold values from 1 to 64
Outputs:
- spectrum: float32 [128, 128, 8, 128], P('bricks', 'frames')
Inputs may be any that keep to these rules, and one draw needn't show every extreme that they name: `counts`: in every frame one brick holds exactly 2048 live atoms; the others hold 1 to 2048.
All inputs are finite; a program needn't handle non-finite values.
Results may differ from a plain program's by a relative error of at most 0.0033.
Values sent between devices are 32-bit elements; how exact they have to be, the bound alone decides.
No kernel may reach another device: no remote copies, remote signals or barrier semaphores. Data moves between devices by JAX's collectives and lax.ppermute only.
A program may use at most 64 MiB of HBM per device.

v0:
```python
import math

import jax
import jax.numpy as jnp
from jax import lax
from jax.sharding import PartitionSpec as P

NW = 128
BLK = 256


def block_factors(coords, valid, wave_x, wave_y, wave_z):
    two_pi = 2.0 * math.pi
    length = coords.shape[1]
    ang_x = two_pi * (coords[0][:, None] * wave_x.astype(jnp.float32)[None, :])
    ang_z = two_pi * (coords[2][:, None] * wave_z.astype(jnp.float32)[None, :])
    cos_x, sin_x = (jnp.cos(ang_x), jnp.sin(ang_x))
    cos_z, sin_z = (jnp.cos(ang_z), jnp.sin(ang_z))
    a_real = cos_x[:, :, None] * cos_z[:, None, :] - sin_x[:, :, None] * sin_z[:, None, :]
    a_imag = -(sin_x[:, :, None] * cos_z[:, None, :] + cos_x[:, :, None] * sin_z[:, None, :])
    left = (
        jnp.concatenate([a_real.reshape(length, -1), a_imag.reshape(length, -1)], axis=1)
        * valid[:, None]
    ).astype(jnp.bfloat16)
    ang_y = two_pi * (coords[1][:, None] * wave_y.astype(jnp.float32)[None, :])
    right = jnp.concatenate([jnp.cos(ang_y), -jnp.sin(ang_y)], axis=1).astype(jnp.bfloat16)
    return (left, right)


def outer_sum(left, right):
    return lax.dot_general(
        left, right, (((0,), (0,)), ((), ())), preferred_element_type=jnp.float32
    )


def combine(accum):
    half = accum.shape[-2] // 2
    cols = accum.shape[-1] // 2
    real_part = accum[..., :half, :cols] - accum[..., half:, cols:]
    imag_part = accum[..., :half, cols:] + accum[..., half:, :cols]
    return jnp.stack([real_part, imag_part], axis=-2)


def to_layout(accum, rows_x, width_z, width_y):
    return jnp.transpose(combine(accum).reshape(rows_x, width_z, 2, width_y), (0, 2, 1, 3))


def block_density(pooled, capacity, low_count, high_count, first, last, wave_x, wave_y, wave_z):
    low_blocks = (low_count + BLK - 1) // BLK
    offsets = jnp.arange(BLK, dtype=jnp.int32)

    def step(item, accum):
        in_low = item < low_blocks
        within = jnp.where(in_low, item, item - low_blocks) * BLK
        offset = jnp.where(in_low, 0, capacity) + within
        limit = jnp.where(in_low, low_count, high_count)
        coords = lax.dynamic_slice(pooled, (jnp.int32(0), offset), (3, BLK))
        valid = (within + offsets < limit).astype(jnp.float32)
        left, right = block_factors(coords, valid, wave_x, wave_y, wave_z)
        return accum + outer_sum(left, right)

    zeros = jnp.zeros((2 * wave_x.shape[0] * wave_z.shape[0], 2 * wave_y.shape[0]), jnp.float32)
    return lax.fori_loop(first, last, step, zeros)


def per_device(positions, counts, kvec_x, kvec_y, kvec_z):
    groups = lax.axis_size("frames")
    bricks = lax.axis_size("bricks")
    brick = lax.axis_index("bricks")
    frames_here = positions.shape[1]
    capacity = positions.shape[2]
    width_x, width_y, width_z = (kvec_x.shape[0], kvec_y.shape[0], kvec_z.shape[0])
    brick_row = jnp.arange(bricks, dtype=jnp.int32)
    own_counts = jnp.sum(jnp.where(brick_row[None, :] == brick, counts, 0), axis=1)
    layers = []
    for frame in range(frames_here):
        blocks_here = (own_counts[frame] + BLK - 1) // BLK
        accum = block_density(
            positions[:, frame],
            capacity,
            own_counts[frame],
            jnp.int32(0),
            jnp.int32(0),
            blocks_here,
            kvec_x,
            kvec_y,
            kvec_z,
        )
        layers.append(to_layout(accum, width_x, width_z, width_y))
    partials = jnp.stack(layers, axis=0)
    density = lax.psum_scatter(partials, "bricks", scatter_dimension=1, tiled=True)
    frames_total = frames_here * groups
    times = jnp.arange(frames_total, dtype=jnp.int32)
    freqs = jnp.arange(NW, dtype=jnp.int32)
    angle = 2.0 * math.pi * (times[:, None] * freqs[None, :] % NW).astype(jnp.float32) / NW
    window = 0.5 - 0.5 * jnp.cos(2.0 * math.pi * (times.astype(jnp.float32) + 0.5) / frames_total)
    cos_table = window[:, None] * jnp.cos(angle)
    sin_table = window[:, None] * jnp.sin(angle)
    norm_total = capacity * bricks * jnp.sum(window * window)
    high = lax.Precision.HIGHEST
    block = lax.all_to_all(density, "frames", split_axis=4, concat_axis=0, tiled=True)
    real_part = block[:, :, 0]
    imag_part = block[:, :, 1]
    re_x = jnp.einsum("tazb,tm->abzm", real_part, cos_table, precision=high) + jnp.einsum(
        "tazb,tm->abzm", imag_part, sin_table, precision=high
    )
    im_x = jnp.einsum("tazb,tm->abzm", imag_part, cos_table, precision=high) - jnp.einsum(
        "tazb,tm->abzm", real_part, sin_table, precision=high
    )
    return (re_x * re_x + im_x * im_x) / norm_total


def solution(mesh):
    return jax.shard_map(
        per_device,
        mesh=mesh,
        in_specs=(P(None, "frames", "bricks"), P("frames", None), P(), P(), P()),
        out_specs=P("bricks", "frames", None, None),
        check_vma=False,
    )
```

profile of v0, /device:TPU:0, one launch (start us, length us, event | category | flops | bytes accessed | tf_op | source)
XLA Modules:
  0.0 224.1 jit_solution(17208220157173694188)
XLA Ops:
  6.5 0.8 select_reduce_fusion
  7.3 0.7 fusion.68
  9.2 0.9 fusion.67
  10.1 0.7 convert_bitcast_fusion.1
  10.8 0.7 convert_bitcast_fusion
  11.5 1.5 broadcast.319.clone.1
  12.9 44.4 %while.28 = (s32[]{:T(128)}, f32[2048,256]{1,0:T(8,128)}, s32[]{:T(128)}, f32[3,2048]{1,0:T(4,128)S(1)}, f32[1,128]{1,0:T(1,128)S(1)}, /*index=5*/f32[1,8]{1,0:T...) while((s32[]{:T(128)}, f32[2048,256]{1,0:T(8,128)}, ...), condition=%wide.region_2.3_spmd.clone, body=%wide.region_1.2_spmd.clone.sunk | while | flops 272864000 | bytes 9220423 | solution.py:63
  13.9 0.6 cosine_convert_fusion.4
  15.1 3.4 %convolution_add_fusion.4 = f32[2048,256]{1,0:T(8,128)} fusion(f32[2048,256]{1,0:T(8,128)} %get-tuple-element.586, f32[256,1024]{0,1:T(8,128)S(1)} %get-tuple-element.505, f32[256,1024]{0,1:T(8,128)S(1)} %get-tuple-element.506, f32[256]{0:T(256)S(1)} %compare_convert_fusion.4, bf16[256,128]{0,1:T(8,128)(2,1)S(1)} %get-tuple-element.508, ...), kind=kOutput, calls=%fused_computation.2.clone.1 | convolution fusion | flops 270794752 | bytes 6423552 | tf_op jit(solution)/shard_map/while/body/dot_general | solution.py:31
  19.5 0.6 cosine_convert_fusion.4
  20.7 3.4 %convolution_add_fusion.4 = f32[2048,256]{1,0:T(8,128)} fusion(f32[2048,256]{1,0:T(8,128)} %get-tuple-element.586, f32[256,1024]{0,1:T(8,128)S(1)} %get-tuple-element.505, f32[256,1024]{0,1:T(8,128)S(1)} %get-tuple-element.506, f32[256]{0:T(256)S(1)} %compare_convert_fusion.4, bf16[256,128]{0,1:T(8,128)(2,1)S(1)} %get-tuple-element.508, ...), kind=kOutput, calls=%fused_computation.2.clone.1 | convolution fusion | flops 270794752 | bytes 6423552 | tf_op jit(solution)/shard_map/while/body/dot_general | solution.py:31
  25.0 0.6 cosine_convert_fusion.4
  26.2 3.4 %convolution_add_fusion.4 = f32[2048,256]{1,0:T(8,128)} fusion(f32[2048,256]{1,0:T(8,128)} %get-tuple-element.586, f32[256,1024]{0,1:T(8,128)S(1)} %get-tuple-element.505, f32[256,1024]{0,1:T(8,128)S(1)} %get-tuple-element.506, f32[256]{0:T(256)S(1)} %compare_convert_fusion.4, bf16[256,128]{0,1:T(8,128)(2,1)S(1)} %get-tuple-element.508, ...), kind=kOutput, calls=%fused_computation.2.clone.1 | convolution fusion | flops 270794752 | bytes 6423552 | tf_op jit(solution)/shard_map/while/body/dot_general | solution.py:31
  30.6 0.6 cosine_convert_fusion.4
  31.8 3.4 %convolution_add_fusion.4 = f32[2048,256]{1,0:T(8,128)} fusion(f32[2048,256]{1,0:T(8,128)} %get-tuple-element.586, f32[256,1024]{0,1:T(8,128)S(1)} %get-tuple-element.505, f32[256,1024]{0,1:T(8,128)S(1)} %get-tuple-element.506, f32[256]{0:T(256)S(1)} %compare_convert_fusion.4, bf16[256,128]{0,1:T(8,128)(2,1)S(1)} %get-tuple-element.508, ...), kind=kOutput, calls=%fused_computation.2.clone.1 | convolution fusion | flops 270794752 | bytes 6423552 | tf_op jit(solution)/shard_map/while/body/dot_general | solution.py:31
  36.2 0.6 cosine_convert_fusion.4
  37.3 3.4 %convolution_add_fusion.4 = f32[2048,256]{1,0:T(8,128)} fusion(f32[2048,256]{1,0:T(8,128)} %get-tuple-element.586, f32[256,1024]{0,1:T(8,128)S(1)} %get-tuple-element.505, f32[256,1024]{0,1:T(8,128)S(1)} %get-tuple-element.506, f32[256]{0:T(256)S(1)} %compare_convert_fusion.4, bf16[256,128]{0,1:T(8,128)(2,1)S(1)} %get-tuple-element.508, ...), kind=kOutput, calls=%fused_computation.2.clone.1 | convolution fusion | flops 270794752 | bytes 6423552 | tf_op jit(solution)/shard_map/while/body/dot_general | solution.py:31
  41.7 0.6 cosine_convert_fusion.4
  42.9 3.4 %convolution_add_fusion.4 = f32[2048,256]{1,0:T(8,128)} fusion(f32[2048,256]{1,0:T(8,128)} %get-tuple-element.586, f32[256,1024]{0,1:T(8,128)S(1)} %get-tuple-element.505, f32[256,1024]{0,1:T(8,128)S(1)} %get-tuple-element.506, f32[256]{0:T(256)S(1)} %compare_convert_fusion.4, bf16[256,128]{0,1:T(8,128)(2,1)S(1)} %get-tuple-element.508, ...), kind=kOutput, calls=%fused_computation.2.clone.1 | convolution fusion | flops 270794752 | bytes 6423552 | tf_op jit(solution)/shard_map/while/body/dot_general | solution.py:31
  47.3 0.6 cosine_convert_fusion.4
  48.4 3.4 %convolution_add_fusion.4 = f32[2048,256]{1,0:T(8,128)} fusion(f32[2048,256]{1,0:T(8,128)} %get-tuple-element.586, f32[256,1024]{0,1:T(8,128)S(1)} %get-tuple-element.505, f32[256,1024]{0,1:T(8,128)S(1)} %get-tuple-element.506, f32[256]{0:T(256)S(1)} %compare_convert_fusion.4, bf16[256,128]{0,1:T(8,128)(2,1)S(1)} %get-tuple-element.508, ...), kind=kOutput, calls=%fused_computation.2.clone.1 | convolution fusion | flops 270794752 | bytes 6423552 | tf_op jit(solution)/shard_map/while/body/dot_general | solution.py:31
  52.8 0.6 cosine_convert_fusion.4
  54.0 3.4 %convolution_add_fusion.4 = f32[2048,256]{1,0:T(8,128)} fusion(f32[2048,256]{1,0:T(8,128)} %get-tuple-element.586, f32[256,1024]{0,1:T(8,128)S(1)} %get-tuple-element.505, f32[256,1024]{0,1:T(8,128)S(1)} %get-tuple-element.506, f32[256]{0:T(256)S(1)} %compare_convert_fusion.4, bf16[256,128]{0,1:T(8,128)(2,1)S(1)} %get-tuple-element.508, ...), kind=kOutput, calls=%fused_computation.2.clone.1 | convolution fusion | flops 270794752 | bytes 6423552 | tf_op jit(solution)/shard_map/while/body/dot_general | solution.py:31
  57.4 1.6 subtract_bitcast_fusion.3
  59.0 1.5 broadcast.319.clone
  60.5 16.8 %while.29 = (s32[]{:T(128)}, f32[2048,256]{1,0:T(8,128)}, s32[]{:T(128)}, f32[3,2048]{1,0:T(4,128)S(1)}, f32[1,128]{1,0:T(1,128)S(1)}, /*index=5*/f32[1,8]{1,0:T...) while((s32[]{:T(128)}, f32[2048,256]{1,0:T(8,128)}, ...), condition=%wide.region_4.5_spmd.clone, body=%wide.region_3.4_spmd.clone.sunk | while | flops 272864000 | bytes 9220423 | solution.py:63
  61.5 0.6 cosine_convert_fusion.5
  62.7 3.4 %convolution_add_fusion.5 = f32[2048,256]{1,0:T(8,128)} fusion(f32[2048,256]{1,0:T(8,128)} %get-tuple-element.544, f32[256,1024]{0,1:T(8,128)S(1)} %get-tuple-element.524, f32[256,1024]{0,1:T(8,128)S(1)} %get-tuple-element.525, f32[256]{0:T(256)S(1)} %compare_convert_fusion.5, bf16[256,128]{0,1:T(8,128)(2,1)S(1)} %get-tuple-element.527, ...), kind=kOutput, calls=%fused_computation.25.clone.1 | convolution fusion | flops 270794752 | bytes 6423552 | tf_op jit(solution)/shard_map/while/body/dot_general | solution.py:31
  68.3 3.4 %convolution_add_fusion.5 = f32[2048,256]{1,0:T(8,128)} fusion(f32[2048,256]{1,0:T(8,128)} %get-tuple-element.544, f32[256,1024]{0,1:T(8,128)S(1)} %get-tuple-element.524, f32[256,1024]{0,1:T(8,128)S(1)} %get-tuple-element.525, f32[256]{0:T(256)S(1)} %compare_convert_fusion.5, bf16[256,128]{0,1:T(8,128)(2,1)S(1)} %get-tuple-element.527, ...), kind=kOutput, calls=%fused_computation.25.clone.1 | convolution fusion | flops 270794752 | bytes 6423552 | tf_op jit(solution)/shard_map/while/body/dot_general | solution.py:31
  73.9 3.4 %convolution_add_fusion.5 = f32[2048,256]{1,0:T(8,128)} fusion(f32[2048,256]{1,0:T(8,128)} %get-tuple-element.544, f32[256,1024]{0,1:T(8,128)S(1)} %get-tuple-element.524, f32[256,1024]{0,1:T(8,128)S(1)} %get-tuple-element.525, f32[256]{0:T(256)S(1)} %compare_convert_fusion.5, bf16[256,128]{0,1:T(8,128)(2,1)S(1)} %get-tuple-element.527, ...), kind=kOutput, calls=%fused_computation.25.clone.1 | convolution fusion | flops 270794752 | bytes 6423552 | tf_op jit(solution)/shard_map/while/body/dot_general | solution.py:31
  77.3 1.6 subtract_bitcast_fusion.2
  79.6 3.0 %copy.42 = f32[16,8,32,128]{3,1,2,0:T(8,128)} copy(f32[16,8,32,128]{3,2,1,0:T(8,128)S(1)} %bitcast.121) | data formatting | bytes 4194304
  82.5 98.6 %reduce-scatter.5.cloned.1.call-done = f32[16,4096]{1,0:T(8,128)} async-done(((f32[128,4096]{1,0:T(8,128)}), f32[16,4096]{1,0:T(8,128)}) %reduce-scatter.5.cloned.1.call-update) | async-done | bytes 262160
  181.1 1.0 copy.38
  182.1 1.9 copy.25
  184.0 1.5 reshape.397
  185.4 3.4 %all-to-all-start = ((f32[4,1,16384]{2,1,0:T(1,128)}), f32[4,1,16384]{2,1,0:T(1,128)S(1)}, u32[]{:S(2)}, u32[]{:S(2)}) async-start(f32[4,1,16384]{2,1,0:T(1,128)} %reshape.397), calls=%async_computation | async-start | bytes 524288 | tf_op jit(solution)/shard_map/all_to_all | solution.py:101
  188.9 0.7 multiply_reduce_fusion
  190.2 4.6 %all-to-all-done = f32[4,1,16384]{2,1,0:T(1,128)S(1)} async-done(((f32[4,1,16384]{2,1,0:T(1,128)}), f32[4,1,16384]{2,1,0:T(1,128)S(1)}, u32[]{:S(2)}, u32[]{:S(2)}) %all-to-all-start) | async-done | bytes 262176 | tf_op jit(solution)/shard_map/all_to_all | solution.py:101
  195.4 1.4 reduce
  196.7 0.7 reshape.398
  197.4 1.8 copy.31
  199.2 0.8 copy.27
  200.1 3.5 %fusion.28 = f32[128,16,8,32]{0,3,2,1:T(8,128)S(1)} fusion(f32[8,16,2,8,32]{4,0,3,1,2:T(8,128)S(1)} %bitcast.122, f32[8]{0:T(128)S(1)} %multiply_subtract_fusion), kind=kOutput, calls=%fused_computation.59 | convolution fusion | flops 50347008 | bytes 2621952 | tf_op jit(solution)/shard_map/tazb,tm->abzm/dot_general | solution.py:104
  203.6 3.5 %fusion.29 = f32[128,16,8,32]{0,3,2,1:T(8,128)S(1)} fusion(f32[8,16,2,8,32]{4,0,3,1,2:T(8,128)S(1)} %bitcast.123, f32[8]{0:T(128)S(1)} %multiply_subtract_fusion), kind=kOutput, calls=%fused_computation.60 | convolution fusion | flops 50347008 | bytes 2621952 | tf_op jit(solution)/shard_map/tazb,tm->abzm/dot_general | solution.py:107
  207.0 3.5 %fusion.30 = f32[128,16,8,32]{0,3,2,1:T(8,128)S(1)} fusion(f32[8,16,2,8,32]{4,0,3,1,2:T(8,128)S(1)} %bitcast.124, f32[8]{0:T(128)S(1)} %multiply_subtract_fusion), kind=kOutput, calls=%fused_computation.61 | convolution fusion | flops 50347008 | bytes 2621952 | tf_op jit(solution)/shard_map/tazb,tm->abzm/dot_general | solution.py:104
  210.5 3.8 %divide_bitcast_fusion = f32[16,32,8,128]{3,1,2,0:T(8,128)S(1)} fusion(f32[128,16,8,32]{0,3,2,1:T(8,128)S(1)} %fusion.29, f32[128,16,8,32]{0,3,2,1:T(8,128)S(1)} %fusion.28, f32[128,16,8,32]{0,3,2,1:T(8,128)S(1)} %fusion.30, f32[]{:T(128)S(6)} %mul_shard_map.3, f32[8,16,2,8,32]{4,0,3,1,2:T(8,128)S(1)} %bitcast.125, f32[8]{0:T(128)S(1)} %multiply_subtract_fusion), kind=kOutput, calls=%fused_computation.50 | convolution fusion | flops 53492736 | bytes 8913412 | tf_op jit(solution)/shard_map/tazb,tm->abzm/dot_general | solution.py:107
  214.3 3.0 %copy.28 = f32[16,32,8,128]{3,2,1,0:T(8,128)} copy(f32[16,32,8,128]{3,1,2,0:T(8,128)S(1)} %divide_bitcast_fusion) | data formatting | bytes 4194304 | tf_op jit(solution)/shard_map/div | solution.py:110
  (67 shorter events, 13.2 us)
Async XLA Ops:
  6.5 174.6 %reduce-scatter.5.cloned.1.call-start = ((), (), s32[]{:S(2)}) async-start(), calls=%async_computation.2 | async-start | bytes 2359296
  185.4 9.4 %all-to-all-start = ((f32[4,1,16384]{2,1,0:T(1,128)}), f32[4,1,16384]{2,1,0:T(1,128)S(1)}, u32[]{:S(2)}, u32[]{:S(2)}) async-start(f32[4,1,16384]{2,1,0:T(1,128)} %reshape.397), calls=%async_computation | async-start | bytes 524288 | tf_op jit(solution)/shard_map/all_to_all | solution.py:101
Sparse Core Ops, SparseCore 0:
  82.7 98.3 reduce-scatter.4
where the time goes:
time: 225 us; the launch traced here: 224 us
  waiting for transfers between devices  103 us (46%)
  matrix products  51.6 us (23%)
  other arithmetic  24.1 us (11%)
  local copies, waits for them, and re-layouts  19.7 us (9%)
  between operations  15.4 us (7%)
  loops' own time  6.82 us (3%)
  starting transfers between devices  3.41 us (2%)
    unnamed x2, waiting for transfers between devices  98.6 us
    dot_general x11, matrix products, outer_sum(): lax.dot_general(left, right, (((0,), (0,)), ((), ())), preferred_element_...  37.3 us
    another operation x2, loops' own time, block_density(): return lax.fori_loop(first, last, step, zeros)  6.82 us
    unnamed x5, local copies, waits for them, and re-layouts  6.4 us
    another operation x11, other arithmetic  6.25 us
    cos x11, other arithmetic, block_factors(): cos_x, sin_x = (jnp.cos(ang_x), jnp.sin(ang_x))  5.9 us
    all_to_all x1, waiting for transfers between devices, per_device(): lax.all_to_all(density, 'frames', split_axis=4, concat_axis=0, tiled=True)  4.61 us
  transfers between devices with their start and end apart: 2, of which 2 were waited for; matrix products, arithmetic and copies ran while one was open for 0% of the time, Pallas kernels for 0%

commit v1 on v0

v1 whole, which is shorter than its diff:
```python
import functools
import math

import jax
import jax.numpy as jnp
import numpy as np
from jax import lax
from jax.experimental import pallas as pl
from jax.experimental.pallas import tpu as pltpu
from jax.sharding import PartitionSpec as P

NW = 128
KMAX = 64
LANES = 128
UNIT = 2

def _fit(fun, degree):
    nodes = 0.125 * (1.0 + np.cos(np.pi * (np.arange(64) + 0.5) / 64))
    series = np.polynomial.chebyshev.Chebyshev.fit(nodes, fun(np.sqrt(nodes)), degree, domain=[0.0, 0.25])
    return [float(c) for c in series.convert(kind=np.polynomial.Polynomial).coef]


COS_C = _fit(lambda f: math.sqrt(2.0) * np.cos(np.pi * f), 4)
SIN_C = _fit(lambda f: math.sqrt(2.0) * np.sin(np.pi * f) / f, 4)


def _poly(coefs, u):
    acc = coefs[-1] * u + coefs[-2]
    for c in coefs[-3::-1]:
        acc = acc * u + c
    return acc


def cis(turns):
    f = turns - jnp.round(turns)
    u = f * f
    half_c = _poly(COS_C, u)
    half_s = _poly(SIN_C, u) * f
    return 1.0 - half_s * half_s, half_s * half_c


def density_kernel(frames, n_x, n_z, dests, counts_ref, me_ref, *refs):
    n_pos = len(frames[1])
    held = frames[1]
    frames_here = frames[0]
    pos_refs = refs[:n_pos]
    kb_ref, ky_ref = refs[n_pos : n_pos + 2]
    outs = refs[n_pos + 2 : n_pos + 2 + dests]
    prod_ref = refs[n_pos + 2 + dests]
    rows = n_x * n_z
    capacity = pos_refs[0].shape[-1]
    step = UNIT * LANES
    me = me_ref[0]
    lane = lax.broadcasted_iota(jnp.int32, (n_z, LANES), 1)

    def factors(pos_ref, shard, frame, offset, count):
        where = pl.ds(pl.multiple_of(offset, LANES), LANES)
        x = pos_ref[shard, 0, pl.ds(frame, 1), where]
        y = pos_ref[shard, 1, pl.ds(frame, 1), where]
        z = pos_ref[shard, 2, pl.ds(frame, 1), where]
        cx, sx = cis(kb_ref[0:n_x, :] * x)
        cz, sz = cis(kb_ref[n_x : n_x + n_z, :] * z)
        cy, sy = cis(kb_ref[n_x + n_z : n_x + n_z + 16, :] * y)
        live = lane + offset < count
        cz = jnp.where(live, cz, 0.0)
        sz = jnp.where(live, sz, 0.0)
        re, im = [], []
        for i in range(n_x):
            a, b = cx[i : i + 1], sx[i : i + 1]
            re.append(a * cz - b * sz)
            im.append(b * cz + a * sz)
        left = jnp.concatenate(re + im, axis=0).astype(jnp.bfloat16)
        ce, se = cy[0:8], sy[0:8]
        re, im = [ce], [se]
        for i in range(8, 15):
            a, b = cy[i : i + 1], sy[i : i + 1]
            re.append(a * ce - b * se)
            im.append(b * ce + a * se)
        right = jnp.concatenate(re + im, axis=0).astype(jnp.bfloat16)
        return left, right

    width = dests * (ky_ref.shape[1] // dests)
    share = width // dests
    ks = lax.broadcasted_iota(jnp.int32, (KMAX, width), 0) + 1
    hot = jnp.where(ks == ky_ref[...], 1.0, 0.0).astype(jnp.bfloat16)
    none = jnp.zeros_like(hot)
    hot = jnp.concatenate(
        [jnp.concatenate([hot, none], axis=1), jnp.concatenate([none, hot], axis=1)], axis=0
    )
    hot = jnp.concatenate([hot, hot, hot], axis=0)

    for frame in range(frames_here):
        prod_ref[...] = jnp.zeros_like(prod_ref)
        for pos_ref, ids in zip(pos_refs, held):
            for shard, distance in enumerate(ids):
                count = counts_ref[frame, me ^ distance]

                def body(block, carry, pos_ref=pos_ref, shard=shard, count=count):
                    parts = [
                        factors(pos_ref, shard, frame, block * step + g * LANES, count)
                        for g in range(UNIT)
                    ]
                    left = jnp.concatenate([p[0] for p in parts], axis=1)
                    right = jnp.concatenate([p[1] for p in parts], axis=1)
                    prod_ref[...] += lax.dot_general(
                        left, right, (((1,), (1,)), ((), ())), preferred_element_type=jnp.float32
                    )
                    return carry

                lax.fori_loop(0, (count + step - 1) // step, body, 0)
        top = prod_ref[0:rows, :]
        low = pltpu.roll(prod_ref[rows : 2 * rows, :], KMAX, 1)
        first = lax.broadcasted_iota(jnp.int32, (rows, 2 * KMAX), 1) < KMAX
        terms = jnp.where(first, top - low, -(top + low))
        hi = terms.astype(jnp.bfloat16)
        rest = terms - hi.astype(jnp.float32)
        mid = rest.astype(jnp.bfloat16)
        tail = (rest - mid.astype(jnp.float32)).astype(jnp.bfloat16)
        split = jnp.concatenate([hi, mid, tail], axis=1)
        picked = lax.dot_general(
            hot, split, (((0,), (1,)), ((), ())), preferred_element_type=jnp.float32
        )
        for part in range(2):
            for dest in range(dests):
                at = part * width + dest * share
                to = (frame * 2 + part) * share
                outs[dest][to : to + share, :] = picked[at : at + share, :]


def spectrum_kernel(groups, share, chunk, n_x, n_z, me_ref, *refs):
    srcs = refs[:groups]
    table_ref, out_ref, all_ref = refs[groups:]
    block = srcs[0].shape[0]
    terms = groups * block // share

    @pl.when(pl.program_id(0) == 0)
    def _():
        for distance in range(groups):
            at = pl.multiple_of((me_ref[0] ^ distance) * block, block)
            all_ref[pl.ds(at, block), :] = srcs[distance][...]

    base = pl.program_id(0) * chunk
    for pair in range(chunk // 2):
        j = base + 2 * pair
        x = jnp.concatenate(
            [all_ref[pl.ds(j + q, terms, stride=share), :] for q in range(2)], axis=0
        )
        hi = x.astype(jnp.bfloat16)
        lo = (x - hi.astype(jnp.float32)).astype(jnp.bfloat16)
        y = lax.dot_general(
            jnp.concatenate([hi, hi, lo], axis=0),
            table_ref[...],
            (((0,), (0,)), ((), ())),
            preferred_element_type=jnp.float32,
        )
        for q in range(2):
            re = y[:, 2 * q * NW : (2 * q + 1) * NW]
            im = y[:, (2 * q + 1) * NW : (2 * q + 2) * NW]
            out_ref[:, 2 * pair + q] = (re * re + im * im).reshape(n_x, n_z, NW)


def dft_table(frames_total, atoms):
    times = jnp.arange(frames_total, dtype=jnp.int32)
    freqs = jnp.arange(NW, dtype=jnp.int32)
    angle = 2.0 * math.pi * (times[:, None] * freqs[None, :] % NW).astype(jnp.float32) / NW
    window = 0.5 - 0.5 * jnp.cos(2.0 * math.pi * (times.astype(jnp.float32) + 0.5) / frames_total)
    scale = lax.rsqrt(atoms * jnp.sum(window * window))
    cw = scale * window[:, None] * jnp.cos(angle)
    sw = scale * window[:, None] * jnp.sin(angle)
    real_row = jnp.concatenate([cw, -sw], axis=1)
    imag_row = jnp.concatenate([sw, cw], axis=1)
    full = jnp.stack([real_row, imag_row], axis=1).reshape(2 * frames_total, 2 * NW)
    none = jnp.zeros_like(full)
    pair = jnp.concatenate(
        [jnp.concatenate([full, none], axis=1), jnp.concatenate([none, full], axis=1)], axis=0
    )
    hi = pair.astype(jnp.bfloat16)
    lo = (pair - hi.astype(jnp.float32)).astype(jnp.bfloat16)
    return jnp.concatenate([hi, lo, hi], axis=0)


def swap(value, axis, size, distance):
    return lax.ppermute(value, axis, [(i, i ^ distance) for i in range(size)])


def per_device(positions, counts, kvec_x, kvec_y, kvec_z):
    groups = lax.axis_size("frames")
    bricks = lax.axis_size("bricks")
    brick = lax.axis_index("bricks")
    group = lax.axis_index("frames")
    frames_here, capacity = positions.shape[1], positions.shape[2]
    n_x, n_z = kvec_x.shape[0] // bricks, kvec_z.shape[0]
    rows = n_x * n_z
    share = kvec_y.shape[0] // groups

    own_x = lax.dynamic_slice(kvec_x, (brick * n_x,), (n_x,))
    waves = jnp.concatenate([own_x, kvec_z, jnp.arange(1, 9), jnp.arange(8, 72, 8)]).astype(jnp.float32)
    kb = jnp.broadcast_to(waves[:, None], (waves.shape[0], LANES))
    order = group ^ jnp.arange(groups, dtype=jnp.int32)
    ky = kvec_y.reshape(groups, share)[order].reshape(1, groups * share)
    table = dft_table(frames_here * groups, capacity * bricks)

    held, ids = positions[None], [0]
    distance = bricks // 2
    while distance:
        got = swap(held, "bricks", bricks, distance)
        held = jnp.concatenate([held, got], axis=0)
        ids = ids + [i ^ distance for i in ids]
        distance //= 2

    vmem = pl.BlockSpec(memory_space=pltpu.VMEM)
    smem = pl.BlockSpec(memory_space=pltpu.SMEM)
    block = frames_here * 2 * share
    sends = pl.pallas_call(
        functools.partial(density_kernel, (frames_here, [ids]), n_x, n_z, groups),
        out_shape=[jax.ShapeDtypeStruct((block, rows), jnp.float32)] * groups,
        in_specs=[smem, smem] + [vmem] * 3,
        out_specs=[vmem] * groups,
        scratch_shapes=[pltpu.VMEM((2 * rows, 2 * KMAX), jnp.float32)],
        name="density",
    )(counts, brick.reshape(1), held, kb, ky)
    got = [sends[0]] + [swap(sends[d], "frames", groups, d) for d in range(1, groups)]

    chunk = min(8, share)
    const = lambda shape: pl.BlockSpec(shape, lambda c: (0, 0))
    return pl.pallas_call(
        functools.partial(spectrum_kernel, groups, share, chunk, n_x, n_z),
        out_shape=jax.ShapeDtypeStruct((n_x, share, n_z, NW), jnp.float32),
        grid=(share // chunk,),
        in_specs=[smem] + [const((block, rows))] * groups + [const(table.shape)],
        out_specs=pl.BlockSpec((n_x, chunk, n_z, NW), lambda c: (0, c, 0, 0)),
        scratch_shapes=[pltpu.VMEM((groups * block, rows), jnp.float32)],
        name="spectrum",
    )(group.reshape(1), *got, table)


def solution(mesh):
    return jax.shard_map(
        per_device,
        mesh=mesh,
        in_specs=(P(None, "frames", "bricks"), P("frames", None), P(), P(), P()),
        out_specs=P("bricks", "frames", None, None),
        check_vma=False,
    )
```

time: 225 us -> 55.6 us (0.25)
  waiting for transfers between devices: 103 us -> 9.98 us
  matrix products: 51.6 us -> 0 us
  Pallas kernels: 0 us -> 22.8 us
  other arithmetic: 24.1 us -> 5.66 us
  local copies, waits for them, and re-layouts: 19.7 us -> 3.95 us
  between operations: 15.4 us -> 0.77 us
  starting transfers between devices: 3.41 us -> 11.6 us
  loops' own time: 6.82 us -> 0 us
    unnamed x2 -> x0, waiting for transfers between devices: 98.6 us -> none
    dot_general x15 -> x0, matrix products: 51.6 us -> none  [the longest x11 37.3 us: outer_sum(): lax.dot_general(left, right, (((0,), (0,)), ((), ())), preferred_element_...]
    pallas_call x0 -> x2, Pallas kernels: none -> 22.8 us  [the longest x1 19.2 us: per_device(): pl.pallas_call(functools.partial(density_kernel, (frames_here, [ids]), n_...]
    ppermute x0 -> x6, starting transfers between devices: none -> 11.6 us  [swap(): return lax.ppermute(value, axis, [(i, i ^ distance) for i in range(size)])]
    ppermute x0 -> x6, waiting for transfers between devices: none -> 9.98 us  [swap(): return lax.ppermute(value, axis, [(i, i ^ distance) for i in range(size)])]
    another operation x16 -> x2, other arithmetic: 9.77 us -> 0.02 us  [dft_table(): jnp.stack([real_row, imag_row], axis=1).reshape(2 * frames_total, 2 * NW)]
    cos x22 -> x0, other arithmetic: 7.21 us -> none  [the longest x11 5.9 us: block_factors(): cos_x, sin_x = (jnp.cos(ang_x), jnp.sin(ang_x))]
    another operation x2 -> x0, loops' own time: 6.82 us -> none  [block_density(): return lax.fori_loop(first, last, step, zeros)]
  transfers between devices with their start and end apart: 2 -> 6, of which waited for: 2 -> 4; matrix products, arithmetic and copies ran while one was open for 0% -> 9% of each run, Pallas kernels for 0% -> 0%
where the time goes in v1:
time: 55.6 us; the launch traced here: 54.8 us
  Pallas kernels  22.8 us (41%)
  starting transfers between devices  11.6 us (21%)
  waiting for transfers between devices  9.98 us (18%)
  other arithmetic  5.66 us (10%)
  local copies, waits for them, and re-layouts  3.95 us (7%)
  between operations  0.77 us (1%)
    pallas_call x1, Pallas kernels, per_device(): pl.pallas_call(functools.partial(density_kernel, (frames_here, [ids]), n_...  19.2 us
    ppermute x6, starting transfers between devices, swap(): return lax.ppermute(value, axis, [(i, i ^ distance) for i in range(size)])  11.6 us
    ppermute x6, waiting for transfers between devices, swap(): return lax.ppermute(value, axis, [(i, i ^ distance) for i in range(size)])  9.98 us
    pallas_call x1, Pallas kernels, per_device(): pl.pallas_call(functools.partial(spectrum_kernel, groups, share, chunk, n...  3.67 us
    concatenate x3, other arithmetic, per_device(): held = jnp.concatenate([held, got], axis=0)  3.47 us
    reshape x2, local copies, waits for them, and re-layouts, per_device(): ky = kvec_y.reshape(groups, share)[order].reshape(1, groups * share)  1.34 us
  transfers between devices with their start and end apart: 6, of which 4 were waited for; matrix products, arithmetic and copies ran while one was open for 9% of the time, Pallas kernels for 0%

profile of v1, /device:TPU:0, one launch (start us, length us, event | category | flops | bytes accessed | tf_op | source)
XLA Modules:
  0.0 54.8 jit_solution(2620357323961156918)
XLA Ops:
  0.0 4.0 %collective-permute-start = (f32[1,3,2,2048]{3,2,1,0:T(2,128)}, f32[1,3,2,2048]{3,2,1,0:T(2,128)S(1)}, u32[]{:S(2)}, u32[]{:S(2)}) collective-permute-start(f32[1,3,2,2048]{3,2,1,0:T(2,128)} %bitcast.7), channel_id=1, source_target_pairs={{0,4},{1,5},{2,6},{3,7},{4,0},{5,1},{6,2},{7,3},{8,12},{9,13},{10,... | collective-permute-start | bytes 147464 | tf_op jit(solution)/shard_map/ppermute | solution.py:183
  4.0 0.6 %multiply_reduce_fusion = f32[]{:T(128)} fusion(), kind=kLoop, calls=%fused_computation.29 | loop fusion | flops 55 | bytes 4 | tf_op jit(solution)/shard_map/reduce_sum | solution.py:167
  5.4 0.1 fusion.7
  5.6 0.7 %reshape.71 = s32[4,32]{1,0:T(4,128)S(1)} reshape(s32[128]{0:T(128)} %param.8) | data formatting | bytes 1024 | tf_op jit(solution)/shard_map/reshape | solution.py:200
  6.4 0.6 %gather_fusion = s32[4,32]{1,0:T(4,128)S(1)} fusion(s32[4,32]{1,0:T(4,128)S(1)} %reshape.71, s32[1024]{0:T(1024)S(1)} %pad_clamp_fusion), kind=kCustom, calls=%fused_computation | custom fusion | bytes 1040 | tf_op jit(solution)/shard_map/gather | solution.py:200
  6.9 0.6 %reshape.72.refs_2_ = s32[1,128]{1,0:T(1,128)} reshape(s32[4,32]{1,0:T(4,128)S(1)} %gather_fusion) | data formatting | bytes 1024 | tf_op jit(solution)/shard_map/reshape | solution.py:200
  7.5 0.7 %dynamic_slice.3 = s32[16]{0:T(128)S(1)} dynamic-slice(s32[128]{0:T(128)} %param.7, s32[]{:T(128)S(6)} %select_n.22), dynamic_slice_sizes={16} | dynamic-slice | bytes 132 | tf_op jit(solution)/shard_map/dynamic_slice | solution.py:196
  8.3 0.0 collective-permute-done
  8.3 0.8 %pad_maximum_fusion.2 = f32[2,3,2,2048]{3,2,1,0:T(2,128)S(1)} fusion(f32[1,3,2,2048]{3,2,1,0:T(2,128)S(1)} %collective-permute-done, f32[1,3,2,2048]{3,2,1,0:T(2,128)} %bitcast.8), kind=kLoop, calls=%fused_computation.3 | loop fusion | flops 24576 | bytes 196608 | tf_op jit(solution)/shard_map/concatenate | solution.py:207
  9.1 1.6 %collective-permute-start.1 = (f32[2,3,2,2048]{3,2,1,0:T(2,128)S(1)}, f32[2,3,2,2048]{3,2,1,0:T(2,128)S(1)}, u32[]{:S(2)}, u32[]{:S(2)}) collective-permute-start(f32[2,3,2,2048]{3,2,1,0:T(2,128)S(1)} %pad_maximum_fusion.2), channel_id=1, source_target_pairs={{0,2},{1,3},{2,0},{3,1},{4,6},{5,7},{6,4},{7,5},{8,10},{9,11},{10,... | collective-permute-start | bytes 294920 | tf_op jit(solution)/shard_map/ppermute | solution.py:183
  10.8 3.0 %collective-permute-done.1 = f32[2,3,2,2048]{3,2,1,0:T(2,128)S(1)} collective-permute-done((f32[2,3,2,2048]{3,2,1,0:T(2,128)S(1)}, f32[2,3,2,2048]{3,2,1,0:T(2,128)S(1)}, u32[]{:S(2)}, u32[]{:S(2)}) %collective-permute-start.1) | collective-permute-done | bytes 98336 | tf_op jit(solution)/shard_map/ppermute | solution.py:183
  13.8 0.9 %pad_maximum_fusion.1 = f32[4,3,2,2048]{3,2,1,0:T(2,128)S(1)} fusion(f32[2,3,2,2048]{3,2,1,0:T(2,128)S(1)} %collective-permute-done.1, f32[1,3,2,2048]{3,2,1,0:T(2,128)S(1)} %collective-permute-done, f32[1,3,2,2048]{3,2,1,0:T(2,128)} %bitcast.9), kind=kLoop, calls=%fused_computation.2 | loop fusion | flops 98304 | bytes 393216 | tf_op jit(solution)/shard_map/concatenate | solution.py:207
  14.7 1.6 %collective-permute-start.2 = (f32[4,3,2,2048]{3,2,1,0:T(2,128)S(1)}, f32[4,3,2,2048]{3,2,1,0:T(2,128)S(1)}, u32[]{:S(2)}, u32[]{:S(2)}) collective-permute-start(f32[4,3,2,2048]{3,2,1,0:T(2,128)S(1)} %pad_maximum_fusion.1), channel_id=1, source_target_pairs={{0,1},{1,0},{2,3},{3,2},{4,5},{5,4},{6,7},{7,6},{8,9},{9,8},{10,11... | collective-permute-start | bytes 589832 | tf_op jit(solution)/shard_map/ppermute | solution.py:183
  16.2 0.7 %add_convert_fusion = f32[40]{0:T(128)S(1)} fusion(s32[8]{0:T(128)S(1)} %get-tuple-element.18, s32[8]{0:T(128)S(1)} %get-tuple-element.19, s32[8]{0:T(128)} %param.9, s32[16]{0:T(128)S(1)} %dynamic_slice.3), kind=kLoop, calls=%fused_computation.28 | loop fusion | flops 160 | bytes 320 | tf_op jit(solution)/shard_map/convert_element_type | solution.py:197
  17.0 3.4 %collective-permute-done.2 = f32[4,3,2,2048]{3,2,1,0:T(2,128)S(1)} collective-permute-done((f32[4,3,2,2048]{3,2,1,0:T(2,128)S(1)}, f32[4,3,2,2048]{3,2,1,0:T(2,128)S(1)}, u32[]{:S(2)}, u32[]{:S(2)}) %collective-permute-start.2) | collective-permute-done | bytes 196640 | tf_op jit(solution)/shard_map/ppermute | solution.py:183
  20.4 1.7 %pad_maximum_fusion.refs_0_ = f32[8,3,2,2048]{3,2,1,0:T(2,128)} fusion(f32[4,3,2,2048]{3,2,1,0:T(2,128)S(1)} %collective-permute-done.2, f32[2,3,2,2048]{3,2,1,0:T(2,128)S(1)} %collective-permute-done.1, f32[1,3,2,2048]{3,2,1,0:T(2,128)S(1)} %collective-permute-done, f32[1,3,2,2048]{3,2,1,0:T(2,128)} %bitcast.10), kind=kLoop, calls=%fused_computation.1 | loop fusion | flops 294912 | bytes 786432 | tf_op jit(solution)/shard_map/concatenate | solution.py:207
  22.2 0.7 %broadcast_in_dim.5.refs_1_ = f32[40,128]{1,0:T(8,128)} broadcast(f32[40]{0:T(128)S(1)} %add_convert_fusion), dimensions={0} | broadcast | bytes 20640 | tf_op jit(solution)/shard_map/broadcast_in_dim | solution.py:198
  22.8 19.2 %density.1 = (f32[128,128]{1,0:T(8,128)}, f32[128,128]{1,0:T(8,128)}, f32[128,128]{1,0:T(8,128)}, f32[128,128]{1,0:T(8,128)}) custom-call(s32[2,8]{1,0:T(2,128)} %counts_ref.1, s32[1]{0:T(128)} %bitcast.1.me_ref, f32[8,3,2,2048]{3,2,1,0:T(2,128)} %pad_maximum_fusion.refs_0_, f32[40,128]{1,0:T(8,128)} %broadcast_in_dim.5.refs_1_, s32[1,128]{1,0:T(1,128)} %reshape.72.refs_2_), custom_call_target="tpu_custom_call" | custom-call | tf_op jit(solution)/shard_map/density/pallas_call | solution.py:214
  42.0 0.0 collective-permute-start.3
  42.0 4.2 %collective-permute-start.4 = (f32[128,128]{1,0:T(8,128)}, f32[128,128]{1,0:T(8,128)S(1)}, u32[]{:S(2)}, u32[]{:S(2)}) collective-permute-start(f32[128,128]{1,0:T(8,128)} %get-tuple-element.11), channel_id=1, source_target_pairs={{0,16},{8,24},{16,0},{24,8},{1,17},{9,25},{17,1},{25,9},{2,18},{10... | collective-permute-start | bytes 196616 | tf_op jit(solution)/shard_map/ppermute | solution.py:183
  46.2 0.1 collective-permute-start.5
  46.4 0.6 %pad_maximum_fusion.3.refs_4_ = bf16[96,512]{1,0:T(8,128)(2,1)} fusion(bf16[32,512]{1,0:T(8,128)(2,1)S(1)} %fusion, bf16[32,512]{1,0:T(8,128)(2,1)S(1)} %subtract_convert_fusion), kind=kLoop, calls=%fused_computation.4 | loop fusion | flops 294912 | bytes 163840 | tf_op jit(solution)/shard_map/concatenate | solution.py:179
  47.0 0.0 collective-permute-done.3.refs_1_
  47.0 0.0 copy-start
  47.0 2.2 %collective-permute-done.4.refs_2_ = f32[128,128]{1,0:T(8,128)S(1)} collective-permute-done((f32[128,128]{1,0:T(8,128)}, f32[128,128]{1,0:T(8,128)S(1)}, u32[]{:S(2)}, u32[]{:S(2)}) %collective-permute-start.4) | collective-permute-done | bytes 65568 | tf_op jit(solution)/shard_map/ppermute | solution.py:183
  49.2 0.0 copy-start.1
  49.2 1.3 %collective-permute-done.5.refs_3_ = f32[128,128]{1,0:T(8,128)S(1)} collective-permute-done((f32[128,128]{1,0:T(8,128)}, f32[128,128]{1,0:T(8,128)S(1)}, u32[]{:S(2)}, u32[]{:S(2)}) %collective-permute-start.5) | collective-permute-done | bytes 65568 | tf_op jit(solution)/shard_map/ppermute | solution.py:183
  50.5 0.0 copy-start.2
  50.5 0.0 copy-done
  50.5 0.0 copy-done.1
  50.5 0.6 %copy-done.2 = f32[128,128]{1,0:T(8,128)} copy-done((f32[128,128]{1,0:T(8,128)}, f32[128,128]{1,0:T(8,128)S(1)}, u32[]{:S(2)}) %copy-start.2) | copy-done | bytes 65560
  51.1 3.7 %spectrum.1 = f32[16,32,8,128]{3,2,1,0:T(8,128)} custom-call(s32[1]{0:T(128)} %bitcast.me_ref, f32[128,128]{1,0:T(8,128)} %get-tuple-element.9.refs_0_, f32[128,128]{1,0:T(8,128)} %copy-done, f32[128,128]{1,0:T(8,128)} %copy-done.1, f32[128,128]{1,0:T(8,128)} %copy-done.2, bf16[96,512]{1,0:T(8,128)(2,1)} %pad_maximum_fusion.3.refs_4_), custom_call_target="tpu_custom_call" | custom-call | tf_op jit(solution)/shard_map/spectrum/pallas_call | solution.py:226
  (11 shorter events, 0.1 us)
Async XLA Ops:
  0.0 8.3 %collective-permute-start = (f32[1,3,2,2048]{3,2,1,0:T(2,128)}, f32[1,3,2,2048]{3,2,1,0:T(2,128)S(1)}, u32[]{:S(2)}, u32[]{:S(2)}) collective-permute-start(f32[1,3,2,2048]{3,2,1,0:T(2,128)} %bitcast.7), channel_id=1, source_target_pairs={{0,4},{1,5},{2,6},{3,7},{4,0},{5,1},{6,2},{7,3},{8,12},{9,13},{10,... | collective-permute-start | bytes 147464 | tf_op jit(solution)/shard_map/ppermute | solution.py:183
  9.1 4.7 %collective-permute-start.1 = (f32[2,3,2,2048]{3,2,1,0:T(2,128)S(1)}, f32[2,3,2,2048]{3,2,1,0:T(2,128)S(1)}, u32[]{:S(2)}, u32[]{:S(2)}) collective-permute-start(f32[2,3,2,2048]{3,2,1,0:T(2,128)S(1)} %pad_maximum_fusion.2), channel_id=1, source_target_pairs={{0,2},{1,3},{2,0},{3,1},{4,6},{5,7},{6,4},{7,5},{8,10},{9,11},{10,... | collective-permute-start | bytes 294920 | tf_op jit(solution)/shard_map/ppermute | solution.py:183
  14.7 5.7 %collective-permute-start.2 = (f32[4,3,2,2048]{3,2,1,0:T(2,128)S(1)}, f32[4,3,2,2048]{3,2,1,0:T(2,128)S(1)}, u32[]{:S(2)}, u32[]{:S(2)}) collective-permute-start(f32[4,3,2,2048]{3,2,1,0:T(2,128)S(1)} %pad_maximum_fusion.1), channel_id=1, source_target_pairs={{0,1},{1,0},{2,3},{3,2},{4,5},{5,4},{6,7},{7,6},{8,9},{9,8},{10,11... | collective-permute-start | bytes 589832 | tf_op jit(solution)/shard_map/ppermute | solution.py:183
  42.0 5.0 %collective-permute-start.3 = (f32[128,128]{1,0:T(8,128)}, f32[128,128]{1,0:T(8,128)S(1)}, u32[]{:S(2)}, u32[]{:S(2)}) collective-permute-start(f32[128,128]{1,0:T(8,128)} %get-tuple-element.10), channel_id=1, source_target_pairs={{0,8},{8,0},{16,24},{24,16},{1,9},{9,1},{17,25},{25,17},{2,10},{10... | collective-permute-start | bytes 196616 | tf_op jit(solution)/shard_map/ppermute | solution.py:183
  42.0 7.2 %collective-permute-start.4 = (f32[128,128]{1,0:T(8,128)}, f32[128,128]{1,0:T(8,128)S(1)}, u32[]{:S(2)}, u32[]{:S(2)}) collective-permute-start(f32[128,128]{1,0:T(8,128)} %get-tuple-element.11), channel_id=1, source_target_pairs={{0,16},{8,24},{16,0},{24,8},{1,17},{9,25},{17,1},{25,9},{2,18},{10... | collective-permute-start | bytes 196616 | tf_op jit(solution)/shard_map/ppermute | solution.py:183
  46.2 4.3 %collective-permute-start.5 = (f32[128,128]{1,0:T(8,128)}, f32[128,128]{1,0:T(8,128)S(1)}, u32[]{:S(2)}, u32[]{:S(2)}) collective-permute-start(f32[128,128]{1,0:T(8,128)} %get-tuple-element.12), channel_id=1, source_target_pairs={{0,24},{8,16},{16,8},{24,0},{1,25},{9,17},{17,9},{25,1},{2,26},{10... | collective-permute-start | bytes 196616 | tf_op jit(solution)/shard_map/ppermute | solution.py:183
  47.0 3.5 %copy-start = (f32[128,128]{1,0:T(8,128)}, f32[128,128]{1,0:T(8,128)S(1)}, u32[]{:S(2)}) copy-start(f32[128,128]{1,0:T(8,128)S(1)} %collective-permute-done.3.refs_1_) | copy-start | bytes 196612
  49.2 1.3 %copy-start.1 = (f32[128,128]{1,0:T(8,128)}, f32[128,128]{1,0:T(8,128)S(1)}, u32[]{:S(2)}) copy-start(f32[128,128]{1,0:T(8,128)S(1)} %collective-permute-done.4.refs_2_) | copy-start | bytes 196612
  50.5 0.6 %copy-start.2 = (f32[128,128]{1,0:T(8,128)}, f32[128,128]{1,0:T(8,128)S(1)}, u32[]{:S(2)}) copy-start(f32[128,128]{1,0:T(8,128)S(1)} %collective-permute-done.5.refs_3_) | copy-start | bytes 196612
